TPU v7x, 256 devices: a whole 4x4x8 slice. The times are simulated.
256 devices in a mesh: rad: 32 (over x, y, core), pol: 8 (over z).
Axes of the slice: x: 4, y: 4, z: 8, core: 2. Of those that a mesh axis runs over, the one named last changes fastest.
Arguments:
- dust: float32 [128, 64, 16384], P(None, 'pol', 'rad'), may hold values from 0.2 to 2
- drift_courant: float32 [128], replicated, may hold values from 0.1 to 0.6
- mixing: float32 [128], replicated, may hold values from 0.02 to 0.1
- pair_table: int32 [3, 2048], replicated, may hold values from 0 to 127
- pair_rate: float32 [2048], replicated, may hold values from 0.002 to 0.02
- absorption: float32 [128, 128], replicated, may hold values from 0.05 to 5
- stellar_flux: float32 [128], replicated, may hold values from 0.01 to 0.1
- band_channel: int32 [128], replicated, may hold values from 0 to 3
Outputs:
- new_dust: float32 [128, 64, 16384], P(None, 'pol', 'rad')
- heating: float32 [4, 64, 16384], P(None, 'pol', 'rad')
Inputs may be any that keep to these rules, and one draw needn't show every extreme that they name: `pair_table`: sizes of dust.
All inputs are finite; a program needn't handle non-finite values.
Results may differ from a plain program's by a relative error of at most 0.00005.
Values sent between devices are 32-bit elements; how exact they have to be, the bound alone decides.
A program may use at most 192 MiB of HBM per device.

v0:
```python
import jax
import jax.numpy as jnp
from jax import lax
from jax.sharding import PartitionSpec as P

CH = 4
depth_scale = 4.0


def padded_2(cells, sides, width):
    for axis, dim in sides:
        count = lax.axis_size(axis)
        ends = count - 1
        head = lax.slice_in_dim(cells, 0, width, axis=dim)
        tail = lax.slice_in_dim(cells, cells.shape[dim] - width, cells.shape[dim], axis=dim)
        cells = jnp.concatenate(
            [
                lax.ppermute(tail, axis, [(i, (i + 1) % count) for i in range(ends)]),
                cells,
                lax.ppermute(head, axis, [((i + 1) % count, i) for i in range(ends)]),
            ],
            axis=dim,
        )
    return cells


def collide(advected, pair_table, pair_rate):
    sizes = advected.shape[0]
    grid = jnp.arange(sizes, dtype=jnp.int32)
    first = pair_table[0]
    second = pair_table[1]
    target = pair_table[2]
    pick_first = (first[:, None] == grid[None, :]).astype(jnp.float32)
    pick_second = (second[:, None] == grid[None, :]).astype(jnp.float32)
    redistribute = (grid[:, None] == target[None, :]).astype(jnp.float32)
    redistribute = redistribute - (grid[:, None] == first[None, :]).astype(jnp.float32)
    redistribute = redistribute - (grid[:, None] == second[None, :]).astype(jnp.float32)

    def one_row(column):
        left_part = jnp.dot(
            pick_first, column, precision=lax.Precision.HIGHEST, preferred_element_type=jnp.float32
        )
        right_part = jnp.dot(
            pick_second, column, precision=lax.Precision.HIGHEST, preferred_element_type=jnp.float32
        )
        product = pair_rate[:, None] * left_part * right_part
        return column + jnp.dot(
            redistribute,
            product,
            precision=lax.Precision.HIGHEST,
            preferred_element_type=jnp.float32,
        )

    rows = lax.map(one_row, jnp.moveaxis(advected, 1, 0))
    return jnp.moveaxis(rows, 0, 1)


def shards(
    dust, drift_courant, mixing, pair_table, pair_rate, absorption, stellar_flux, band_channel
):
    padded = padded_2(dust, (("rad", 2), ("pol", 1)), 1)
    center = padded[:, 1:-1, 1:-1]
    outer = padded[:, 1:-1, 2:]
    inner = padded[:, 1:-1, :-2]
    upper = padded[:, 2:, 1:-1]
    lower = padded[:, :-2, 1:-1]
    drift = drift_courant[:, None, None]
    spread = mixing[:, None, None]
    advected = (
        center + drift * (outer - center) + spread * (outer + inner + upper + lower - 4.0 * center)
    )
    new_dust = collide(advected, pair_table, pair_rate)
    sizes = absorption.shape[1]
    opacity = (
        jnp.einsum("bs,str->btr", absorption, new_dust, precision=lax.Precision.HIGHEST) / sizes
    )
    tile = dust.shape[2]
    rad_count = lax.axis_size("rad")
    ray_length = tile * rad_count
    cell_index = jnp.arange(tile, dtype=jnp.int32)
    strict_upper = (cell_index[:, None] < cell_index[None, :]).astype(jnp.float32)
    channels = jnp.arange(CH, dtype=jnp.int32)
    ray_block = lax.all_to_all(opacity, "rad", split_axis=0, concat_axis=2, tiled=True)
    local_bands = ray_block.shape[0]
    polar_rows = ray_block.shape[1]
    first_band = lax.axis_index("rad") * local_bands
    step_depth = ray_block * (depth_scale / ray_length)
    pieces = step_depth.reshape(local_bands, polar_rows, rad_count, tile)
    within = jnp.einsum("bkni,ij->bknj", pieces, strict_upper, precision=lax.Precision.HIGHEST)
    totals = jnp.sum(pieces, axis=3)
    offsets = jnp.cumsum(totals, axis=2) - totals
    depth = (within + offsets[..., None]).reshape(step_depth.shape)
    flux_part = lax.dynamic_slice_in_dim(stellar_flux, first_band, local_bands)
    channel_part = lax.dynamic_slice_in_dim(band_channel, first_band, local_bands)
    absorbed = flux_part[:, None, None] * jnp.exp(-depth) * -jnp.expm1(-step_depth) * ray_length
    picker = (channels[:, None] == channel_part[None, :]).astype(jnp.float32)
    partial_heat = jnp.einsum("cb,bkr->ckr", picker, absorbed, precision=lax.Precision.HIGHEST)
    heating = lax.psum_scatter(partial_heat, "rad", scatter_dimension=2, tiled=True)
    return (new_dust, heating)


def solution(mesh):
    placed = (P(None, "pol", "rad"), P(), P(), P(), P(), P(), P(), P())
    return jax.shard_map(
        shards,
        mesh=mesh,
        in_specs=placed,
        out_specs=(P(None, "pol", "rad"), P(None, "pol", "rad")),
        check_vma=False,
    )
```

profile of v0, /device:TPU:32, one launch (start us, length us, event | category | flops | bytes accessed | tf_op | source)
XLA Modules:
  0.0 392.9 jit_solution(9531429614701989408)
XLA Ops:
  30.5 118.0 %while.12 = (s32[]{:T(128)}, f32[8,128,512]{1,2,0:T(8,128)}, f32[8,128,512]{1,2,0:T(8,128)}, f32[2048]{0:T(1024)S(1)}, s32[2048]{0:T(1024)S(1)}, /*index=5*/s32[2048]{0:T(1024)S(1)}, s32[2048]{0:T(1024)S(1)}, s32[]{:T(128)}) while((s32[]{:T(128)}, f32[8,128,512]{1,2,0:T(8,128)}, f32[8,128,512]{1,2,0:T(8,128)}, ...), condition=%wide.region_1.2_spmd.clone.clone, body=%wide.region_0.1_spmd.clone.clone.sunk | while | flops 4837146624 | bytes 17875048 | solution.py:54
  30.5 4.6 %fusion.86 = f32[512,2048]{1,0:T(8,128)S(1)} fusion(s32[2048]{0:T(1024)S(1)} %get-tuple-element.184, f32[8,128,512]{1,2,0:T(8,128)} %get-tuple-element.181, s32[]{:T(128)S(6)} %copy.88), kind=kOutput, calls=%fused_computation.19.clone.1 | convolution fusion | flops 1611137024 | bytes 4464644 | tf_op jit(solution)/shard_map/while/body/eval_jaxpr/dot_general | solution.py:43
  35.1 4.6 %fusion.87 = f32[512,2048]{1,0:T(8,128)S(1)} fusion(s32[2048]{0:T(1024)S(1)} %get-tuple-element.183, f32[8,128,512]{1,2,0:T(8,128)} %get-tuple-element.181, s32[]{:T(128)S(6)} %copy.88), kind=kOutput, calls=%fused_computation.22.clone.1 | convolution fusion | flops 1611137024 | bytes 4464644 | tf_op jit(solution)/shard_map/while/body/eval_jaxpr/dot_general | solution.py:40
  39.7 5.6 %fusion.88 = f32[8,128,512]{1,2,0:T(8,128)} fusion(f32[8,128,512]{1,2,0:T(8,128)} %get-tuple-element.172, s32[]{:T(128)S(6)} %copy.88, f32[512,2048]{1,0:T(8,128)S(1)} %fusion.86, f32[512,2048]{1,0:T(8,128)S(1)} %fusion.87, f32[2048]{0:T(1024)S(1)} %get-tuple-element.182, s32[2048]{0:T(1024)S(1)} %get-tuple-element.184, ...), kind=kOutput, calls=%fused_computation.10.clone.1 | convolution fusion | flops 1614872576 | bytes 8945668 | tf_op jit(solution)/shard_map/while/body/eval_jaxpr/dot_general | solution.py:47
  49.9 4.6 %fusion.87 = f32[512,2048]{1,0:T(8,128)S(1)} fusion(s32[2048]{0:T(1024)S(1)} %get-tuple-element.183, f32[8,128,512]{1,2,0:T(8,128)} %get-tuple-element.181, s32[]{:T(128)S(6)} %copy.88), kind=kOutput, calls=%fused_computation.22.clone.1 | convolution fusion | flops 1611137024 | bytes 4464644 | tf_op jit(solution)/shard_map/while/body/eval_jaxpr/dot_general | solution.py:40
  54.5 5.6 %fusion.88 = f32[8,128,512]{1,2,0:T(8,128)} fusion(f32[8,128,512]{1,2,0:T(8,128)} %get-tuple-element.172, s32[]{:T(128)S(6)} %copy.88, f32[512,2048]{1,0:T(8,128)S(1)} %fusion.86, f32[512,2048]{1,0:T(8,128)S(1)} %fusion.87, f32[2048]{0:T(1024)S(1)} %get-tuple-element.182, s32[2048]{0:T(1024)S(1)} %get-tuple-element.184, ...), kind=kOutput, calls=%fused_computation.10.clone.1 | convolution fusion | flops 1614872576 | bytes 8945668 | tf_op jit(solution)/shard_map/while/body/eval_jaxpr/dot_general | solution.py:47
  64.6 4.6 %fusion.87 = f32[512,2048]{1,0:T(8,128)S(1)} fusion(s32[2048]{0:T(1024)S(1)} %get-tuple-element.183, f32[8,128,512]{1,2,0:T(8,128)} %get-tuple-element.181, s32[]{:T(128)S(6)} %copy.88), kind=kOutput, calls=%fused_computation.22.clone.1 | convolution fusion | flops 1611137024 | bytes 4464644 | tf_op jit(solution)/shard_map/while/body/eval_jaxpr/dot_general | solution.py:40
  69.2 5.6 %fusion.88 = f32[8,128,512]{1,2,0:T(8,128)} fusion(f32[8,128,512]{1,2,0:T(8,128)} %get-tuple-element.172, s32[]{:T(128)S(6)} %copy.88, f32[512,2048]{1,0:T(8,128)S(1)} %fusion.86, f32[512,2048]{1,0:T(8,128)S(1)} %fusion.87, f32[2048]{0:T(1024)S(1)} %get-tuple-element.182, s32[2048]{0:T(1024)S(1)} %get-tuple-element.184, ...), kind=kOutput, calls=%fused_computation.10.clone.1 | convolution fusion | flops 1614872576 | bytes 8945668 | tf_op jit(solution)/shard_map/while/body/eval_jaxpr/dot_general | solution.py:47
  74.8 4.6 %fusion.86 = f32[512,2048]{1,0:T(8,128)S(1)} fusion(s32[2048]{0:T(1024)S(1)} %get-tuple-element.184, f32[8,128,512]{1,2,0:T(8,128)} %get-tuple-element.181, s32[]{:T(128)S(6)} %copy.88), kind=kOutput, calls=%fused_computation.19.clone.1 | convolution fusion | flops 1611137024 | bytes 4464644 | tf_op jit(solution)/shard_map/while/body/eval_jaxpr/dot_general | solution.py:43
  79.4 4.6 %fusion.87 = f32[512,2048]{1,0:T(8,128)S(1)} fusion(s32[2048]{0:T(1024)S(1)} %get-tuple-element.183, f32[8,128,512]{1,2,0:T(8,128)} %get-tuple-element.181, s32[]{:T(128)S(6)} %copy.88), kind=kOutput, calls=%fused_computation.22.clone.1 | convolution fusion | flops 1611137024 | bytes 4464644 | tf_op jit(solution)/shard_map/while/body/eval_jaxpr/dot_general | solution.py:40
  84.0 5.6 %fusion.88 = f32[8,128,512]{1,2,0:T(8,128)} fusion(f32[8,128,512]{1,2,0:T(8,128)} %get-tuple-element.172, s32[]{:T(128)S(6)} %copy.88, f32[512,2048]{1,0:T(8,128)S(1)} %fusion.86, f32[512,2048]{1,0:T(8,128)S(1)} %fusion.87, f32[2048]{0:T(1024)S(1)} %get-tuple-element.182, s32[2048]{0:T(1024)S(1)} %get-tuple-element.184, ...), kind=kOutput, calls=%fused_computation.10.clone.1 | convolution fusion | flops 1614872576 | bytes 8945668 | tf_op jit(solution)/shard_map/while/body/eval_jaxpr/dot_general | solution.py:47
  94.1 4.6 %fusion.87 = f32[512,2048]{1,0:T(8,128)S(1)} fusion(s32[2048]{0:T(1024)S(1)} %get-tuple-element.183, f32[8,128,512]{1,2,0:T(8,128)} %get-tuple-element.181, s32[]{:T(128)S(6)} %copy.88), kind=kOutput, calls=%fused_computation.22.clone.1 | convolution fusion | flops 1611137024 | bytes 4464644 | tf_op jit(solution)/shard_map/while/body/eval_jaxpr/dot_general | solution.py:40
  98.7 5.6 %fusion.88 = f32[8,128,512]{1,2,0:T(8,128)} fusion(f32[8,128,512]{1,2,0:T(8,128)} %get-tuple-element.172, s32[]{:T(128)S(6)} %copy.88, f32[512,2048]{1,0:T(8,128)S(1)} %fusion.86, f32[512,2048]{1,0:T(8,128)S(1)} %fusion.87, f32[2048]{0:T(1024)S(1)} %get-tuple-element.182, s32[2048]{0:T(1024)S(1)} %get-tuple-element.184, ...), kind=kOutput, calls=%fused_computation.10.clone.1 | convolution fusion | flops 1614872576 | bytes 8945668 | tf_op jit(solution)/shard_map/while/body/eval_jaxpr/dot_general | solution.py:47
  108.9 4.6 %fusion.87 = f32[512,2048]{1,0:T(8,128)S(1)} fusion(s32[2048]{0:T(1024)S(1)} %get-tuple-element.183, f32[8,128,512]{1,2,0:T(8,128)} %get-tuple-element.181, s32[]{:T(128)S(6)} %copy.88), kind=kOutput, calls=%fused_computation.22.clone.1 | convolution fusion | flops 1611137024 | bytes 4464644 | tf_op jit(solution)/shard_map/while/body/eval_jaxpr/dot_general | solution.py:40
  113.5 5.6 %fusion.88 = f32[8,128,512]{1,2,0:T(8,128)} fusion(f32[8,128,512]{1,2,0:T(8,128)} %get-tuple-element.172, s32[]{:T(128)S(6)} %copy.88, f32[512,2048]{1,0:T(8,128)S(1)} %fusion.86, f32[512,2048]{1,0:T(8,128)S(1)} %fusion.87, f32[2048]{0:T(1024)S(1)} %get-tuple-element.182, s32[2048]{0:T(1024)S(1)} %get-tuple-element.184, ...), kind=kOutput, calls=%fused_computation.10.clone.1 | convolution fusion | flops 1614872576 | bytes 8945668 | tf_op jit(solution)/shard_map/while/body/eval_jaxpr/dot_general | solution.py:47
  123.6 4.6 %fusion.87 = f32[512,2048]{1,0:T(8,128)S(1)} fusion(s32[2048]{0:T(1024)S(1)} %get-tuple-element.183, f32[8,128,512]{1,2,0:T(8,128)} %get-tuple-element.181, s32[]{:T(128)S(6)} %copy.88), kind=kOutput, calls=%fused_computation.22.clone.1 | convolution fusion | flops 1611137024 | bytes 4464644 | tf_op jit(solution)/shard_map/while/body/eval_jaxpr/dot_general | solution.py:40
  128.3 5.6 %fusion.88 = f32[8,128,512]{1,2,0:T(8,128)} fusion(f32[8,128,512]{1,2,0:T(8,128)} %get-tuple-element.172, s32[]{:T(128)S(6)} %copy.88, f32[512,2048]{1,0:T(8,128)S(1)} %fusion.86, f32[512,2048]{1,0:T(8,128)S(1)} %fusion.87, f32[2048]{0:T(1024)S(1)} %get-tuple-element.182, s32[2048]{0:T(1024)S(1)} %get-tuple-element.184, ...), kind=kOutput, calls=%fused_computation.10.clone.1 | convolution fusion | flops 1614872576 | bytes 8945668 | tf_op jit(solution)/shard_map/while/body/eval_jaxpr/dot_general | solution.py:47
  138.4 4.6 %fusion.87 = f32[512,2048]{1,0:T(8,128)S(1)} fusion(s32[2048]{0:T(1024)S(1)} %get-tuple-element.183, f32[8,128,512]{1,2,0:T(8,128)} %get-tuple-element.181, s32[]{:T(128)S(6)} %copy.88), kind=kOutput, calls=%fused_computation.22.clone.1 | convolution fusion | flops 1611137024 | bytes 4464644 | tf_op jit(solution)/shard_map/while/body/eval_jaxpr/dot_general | solution.py:40
  143.0 5.6 %fusion.88 = f32[8,128,512]{1,2,0:T(8,128)} fusion(f32[8,128,512]{1,2,0:T(8,128)} %get-tuple-element.172, s32[]{:T(128)S(6)} %copy.88, f32[512,2048]{1,0:T(8,128)S(1)} %fusion.86, f32[512,2048]{1,0:T(8,128)S(1)} %fusion.87, f32[2048]{0:T(1024)S(1)} %get-tuple-element.182, s32[2048]{0:T(1024)S(1)} %get-tuple-element.184, ...), kind=kOutput, calls=%fused_computation.10.clone.1 | convolution fusion | flops 1614872576 | bytes 8945668 | tf_op jit(solution)/shard_map/while/body/eval_jaxpr/dot_general | solution.py:47
  154.0 9.3 %all-to-all-start = ((f32[128,8,512]{2,1,0:T(8,128)}), f32[128,8,512]{2,1,0:T(8,128)}, u32[]{:S(2)}, u32[]{:S(2)}) async-start(f32[128,8,512]{2,1,0:T(8,128)} %copy.65), calls=%async_computation | async-start | bytes 4194304 | tf_op jit(solution)/shard_map/all_to_all | solution.py:83
  163.5 28.7 %all-to-all-done = f32[128,8,512]{2,1,0:T(8,128)} async-done(((f32[128,8,512]{2,1,0:T(8,128)}), f32[128,8,512]{2,1,0:T(8,128)}, u32[]{:S(2)}, u32[]{:S(2)}) %all-to-all-start) | async-done | bytes 2097184 | tf_op jit(solution)/shard_map/all_to_all | solution.py:83
  210.2 30.8 %copy.72 = f32[4,8,16384]{0,1,2:T(8,128)} copy(f32[4,8,16384]{2,0,1:T(4,128)S(1)} %fusion.56) | data formatting | bytes 4194304
  241.0 41.7 %reshape.39 = f32[16384,32]{1,0:T(8,128)} reshape(f32[16384,8,4]{2,1,0:T(8,128)} %bitcast.19) | data formatting | bytes 4194304
  286.2 96.8 %reduce-scatter.4.cloned.1.call-done = f32[512,32]{1,0:T(8,128)} async-done(((f32[16384,32]{1,0:T(8,128)}), f32[512,32]{1,0:T(8,128)}) %reduce-scatter.4.cloned.1.call-update) | async-done | bytes 65552
  (56 shorter events, 80.9 us)
Async XLA Ops:
  7.2 141.4 %copy-start = (f32[128,128]{1,0:T(8,128)S(1)}, f32[128,128]{1,0:T(8,128)}, u32[]{:S(2)}) copy-start(f32[128,128]{1,0:T(8,128)} %param.15) | copy-start | bytes 196612
  9.2 12.1 %copy-start.4 = (s32[3,2048]{1,0:T(4,128)S(1)}, s32[3,2048]{1,0:T(4,128)}, u32[]{:S(2)}) copy-start(s32[3,2048]{1,0:T(4,128)} %param.13) | copy-start | bytes 73732
  9.2 18.1 %copy-start.5 = (f32[128]{0:T(128)S(1)}, f32[128]{0:T(128)}, u32[]{:S(2)}) copy-start(f32[128]{0:T(128)} %param.12) | copy-start | bytes 1540
  9.2 18.1 %copy-start.6 = (f32[128]{0:T(128)S(1)}, f32[128]{0:T(128)}, u32[]{:S(2)}) copy-start(f32[128]{0:T(128)} %param.11) | copy-start | bytes 1540
  9.3 3.1 collective-permute-start.1
  11.0 4.4 %collective-permute-start = (f32[128,8,1]{0,2,1:T(1,128)S(1)}, f32[128,8,1]{0,2,1:T(1,128)S(1)}, u32[]{:S(2)}, u32[]{:S(2)}) collective-permute-start(f32[128,8,1]{0,2,1:T(1,128)S(1)} %get-tuple-element.116), channel_id=1, source_target_pairs={{8,0},{16,8},{24,16},{32,24},{40,32},{48,40},{56,48},{64,56},{72,6... | collective-permute-start | bytes 12296 | tf_op jit(solution)/shard_map/ppermute | solution.py:20
  15.5 9.6 %collective-permute-start.2 = (f32[128,1,514]{0,2,1:T(8,128)S(1)}, f32[128,1,514]{0,2,1:T(8,128)S(1)}, u32[]{:S(2)}, u32[]{:S(2)}) collective-permute-start(f32[128,1,514]{0,2,1:T(8,128)S(1)} %get-tuple-element.111), channel_id=1, source_target_pairs={{1,0},{2,1},{3,2},{4,3},{5,4},{6,5},{7,6},{9,8},{10,9},{11,10},{12... | collective-permute-start | bytes 789512 | tf_op jit(solution)/shard_map/ppermute | solution.py:20
  17.5 9.9 %collective-permute-start.3 = (f32[128,1,514]{0,2,1:T(8,128)S(1)}, f32[128,1,514]{0,2,1:T(8,128)S(1)}, u32[]{:S(2)}, u32[]{:S(2)}) collective-permute-start(f32[128,1,514]{0,2,1:T(8,128)S(1)} %get-tuple-element.112), channel_id=1, source_target_pairs={{0,1},{1,2},{2,3},{3,4},{4,5},{5,6},{6,7},{8,9},{9,10},{10,11},{11... | collective-permute-start | bytes 789512 | tf_op jit(solution)/shard_map/ppermute | solution.py:18
  21.4 9.2 %copy-start.3 = (f32[2048]{0:T(1024)S(1)}, f32[2048]{0:T(1024)}, u32[]{:S(2)}) copy-start(f32[2048]{0:T(1024)} %param.14) | copy-start | bytes 24580
  154.0 9.4 %copy-start.7 = (f32[128]{0:T(128)S(1)}, f32[128]{0:T(128)}, u32[]{:S(2)}) copy-start(f32[128]{0:T(128)} %param.16) | copy-start | bytes 1540
  154.0 9.5 %copy-start.8 = (s32[128]{0:T(128)S(1)}, s32[128]{0:T(128)}, u32[]{:S(2)}) copy-start(s32[128]{0:T(128)} %param.17) | copy-start | bytes 1540
  154.0 38.2 %all-to-all-start = ((f32[128,8,512]{2,1,0:T(8,128)}), f32[128,8,512]{2,1,0:T(8,128)}, u32[]{:S(2)}, u32[]{:S(2)}) async-start(f32[128,8,512]{2,1,0:T(8,128)} %copy.65), calls=%async_computation | async-start | bytes 4194304 | tf_op jit(solution)/shard_map/all_to_all | solution.py:83
  163.3 219.7 %reduce-scatter.4.cloned.1.call-start = ((), (), s32[]{:S(2)}) async-start(), calls=%async_computation.2 | async-start | bytes 8650752
  202.2 2.9 copy-start.1
  282.7 1.6 copy-start.2
Sparse Core Ops, SparseCore 0:
  282.8 100.1 reduce-scatter.3
where the time goes:
time: 395 us; the launch traced here: 393 us
  waiting for transfers between devices  135 us (34%)
  matrix products  129 us (33%)
  local copies, waits for them, and re-layouts  87.7 us (22%)
  starting transfers between devices  18.2 us (5%)
  between operations  14.2 us (4%)
  other arithmetic  9.31 us (2%)
    unnamed x2, waiting for transfers between devices  96.8 us
    unnamed x23, local copies, waits for them, and re-layouts  79.1 us
    dot_general x8, matrix products, one_row(): jnp.dot(redistribute, product, precision=lax.Precision.HIGHEST, preferred...  44.4 us
    dot_general x8, matrix products, one_row(): jnp.dot(pick_first, column, precision=lax.Precision.HIGHEST, preferred_el...  36.8 us
    dot_general x8, matrix products, one_row(): jnp.dot(pick_second, column, precision=lax.Precision.HIGHEST, preferred_e...  36.7 us
    all_to_all x1, waiting for transfers between devices, shards(): lax.all_to_all(opacity, 'rad', split_axis=0, concat_axis=2, tiled=True)  28.7 us
    all_to_all x1, starting transfers between devices, shards(): lax.all_to_all(opacity, 'rad', split_axis=0, concat_axis=2, tiled=True)  9.3 us
  transfers between devices with their start and end apart: 6, of which 5 were waited for; matrix products, arithmetic and copies ran while one was open for 1% of the time, Pallas kernels for 0%

commit v1 on v0

--- a/solution.py
+++ b/solution.py
@@ -80,7 +80,10 @@
     cell_index = jnp.arange(tile, dtype=jnp.int32)
     strict_upper = (cell_index[:, None] < cell_index[None, :]).astype(jnp.float32)
     channels = jnp.arange(CH, dtype=jnp.int32)
-    ray_block = lax.all_to_all(opacity, "rad", split_axis=0, concat_axis=2, tiled=True)
+    ray_block = jnp.concatenate(
+        lax.all_to_all(jnp.stack(jnp.split(opacity, lax.axis_size("rad"), axis=0)), "rad", 0, 0),
+        axis=2,
+    )
     local_bands = ray_block.shape[0]
     polar_rows = ray_block.shape[1]
     first_band = lax.axis_index("rad") * local_bands

time: 395 us -> 417 us (1.056)
  local copies, waits for them, and re-layouts: 87.7 us -> 110 us
    unnamed x23 -> x56, local copies, waits for them, and re-layouts: 79.1 us -> 98.6 us
where the time goes in v1:
time: 417 us; the launch traced here: 415 us
  waiting for transfers between devices  135 us (32%)
  matrix products  129 us (31%)
  local copies, waits for them, and re-layouts  110 us (26%)
  starting transfers between devices  18.1 us (4%)
  between operations  14.2 us (3%)
  other arithmetic  9.09 us (2%)
    unnamed x56, local copies, waits for them, and re-layouts  98.6 us
    unnamed x2, waiting for transfers between devices  96.8 us
    dot_general x8, matrix products, one_row(): jnp.dot(redistribute, product, precision=lax.Precision.HIGHEST, preferred...  44.4 us
    dot_general x8, matrix products, one_row(): jnp.dot(pick_first, column, precision=lax.Precision.HIGHEST, preferred_el...  36.8 us
    dot_general x8, matrix products, one_row(): jnp.dot(pick_second, column, precision=lax.Precision.HIGHEST, preferred_e...  36.7 us
    all_to_all x1, waiting for transfers between devices, shards(): lax.all_to_all(jnp.stack(jnp.split(opacity, lax.axis_size('rad'), axis=0)...  28.7 us
    all_to_all x1, starting transfers between devices, shards(): lax.all_to_all(jnp.stack(jnp.split(opacity, lax.axis_size('rad'), axis=0)...  9.17 us
  transfers between devices with their start and end apart: 6, of which 5 were waited for; matrix products, arithmetic and copies ran while one was open for 1% of the time, Pallas kernels for 0%

profile of v1, /device:TPU:32, one launch (start us, length us, event | category | flops | bytes accessed | tf_op | source)
XLA Modules:
  0.0 414.9 jit_solution(971978626956984667)
XLA Ops:
  30.5 118.0 %while.12 = (s32[]{:T(128)}, f32[8,128,512]{1,2,0:T(8,128)}, f32[8,128,512]{1,2,0:T(8,128)}, f32[2048]{0:T(1024)S(1)}, s32[2048]{0:T(1024)S(1)}, /*index=5*/s32[2048]{0:T(1024)S(1)}, s32[2048]{0:T(1024)S(1)}, s32[]{:T(128)}) while((s32[]{:T(128)}, f32[8,128,512]{1,2,0:T(8,128)}, f32[8,128,512]{1,2,0:T(8,128)}, ...), condition=%wide.region_1.2_spmd.clone.clone, body=%wide.region_0.1_spmd.clone.clone.sunk | while | flops 4837146624 | bytes 17875048 | solution.py:54
  30.5 4.6 %fusion.86 = f32[512,2048]{1,0:T(8,128)S(1)} fusion(s32[2048]{0:T(1024)S(1)} %get-tuple-element.182, f32[8,128,512]{1,2,0:T(8,128)} %get-tuple-element.179, s32[]{:T(128)S(6)} %copy.67), kind=kOutput, calls=%fused_computation.19.clone.1 | convolution fusion | flops 1611137024 | bytes 4464644 | tf_op jit(solution)/shard_map/while/body/eval_jaxpr/dot_general | solution.py:43
  35.1 4.6 %fusion.87 = f32[512,2048]{1,0:T(8,128)S(1)} fusion(s32[2048]{0:T(1024)S(1)} %get-tuple-element.181, f32[8,128,512]{1,2,0:T(8,128)} %get-tuple-element.179, s32[]{:T(128)S(6)} %copy.67), kind=kOutput, calls=%fused_computation.22.clone.1 | convolution fusion | flops 1611137024 | bytes 4464644 | tf_op jit(solution)/shard_map/while/body/eval_jaxpr/dot_general | solution.py:40
  39.7 5.6 %fusion.88 = f32[8,128,512]{1,2,0:T(8,128)} fusion(f32[8,128,512]{1,2,0:T(8,128)} %get-tuple-element.170, s32[]{:T(128)S(6)} %copy.67, f32[512,2048]{1,0:T(8,128)S(1)} %fusion.86, f32[512,2048]{1,0:T(8,128)S(1)} %fusion.87, f32[2048]{0:T(1024)S(1)} %get-tuple-element.180, s32[2048]{0:T(1024)S(1)} %get-tuple-element.182, ...), kind=kOutput, calls=%fused_computation.10.clone.1 | convolution fusion | flops 1614872576 | bytes 8945668 | tf_op jit(solution)/shard_map/while/body/eval_jaxpr/dot_general | solution.py:47
  49.8 4.6 %fusion.87 = f32[512,2048]{1,0:T(8,128)S(1)} fusion(s32[2048]{0:T(1024)S(1)} %get-tuple-element.181, f32[8,128,512]{1,2,0:T(8,128)} %get-tuple-element.179, s32[]{:T(128)S(6)} %copy.67), kind=kOutput, calls=%fused_computation.22.clone.1 | convolution fusion | flops 1611137024 | bytes 4464644 | tf_op jit(solution)/shard_map/while/body/eval_jaxpr/dot_general | solution.py:40
  54.4 5.6 %fusion.88 = f32[8,128,512]{1,2,0:T(8,128)} fusion(f32[8,128,512]{1,2,0:T(8,128)} %get-tuple-element.170, s32[]{:T(128)S(6)} %copy.67, f32[512,2048]{1,0:T(8,128)S(1)} %fusion.86, f32[512,2048]{1,0:T(8,128)S(1)} %fusion.87, f32[2048]{0:T(1024)S(1)} %get-tuple-element.180, s32[2048]{0:T(1024)S(1)} %get-tuple-element.182, ...), kind=kOutput, calls=%fused_computation.10.clone.1 | convolution fusion | flops 1614872576 | bytes 8945668 | tf_op jit(solution)/shard_map/while/body/eval_jaxpr/dot_general | solution.py:47
  60.0 4.6 %fusion.86 = f32[512,2048]{1,0:T(8,128)S(1)} fusion(s32[2048]{0:T(1024)S(1)} %get-tuple-element.182, f32[8,128,512]{1,2,0:T(8,128)} %get-tuple-element.179, s32[]{:T(128)S(6)} %copy.67), kind=kOutput, calls=%fused_computation.19.clone.1 | convolution fusion | flops 1611137024 | bytes 4464644 | tf_op jit(solution)/shard_map/while/body/eval_jaxpr/dot_general | solution.py:43
  64.6 4.6 %fusion.87 = f32[512,2048]{1,0:T(8,128)S(1)} fusion(s32[2048]{0:T(1024)S(1)} %get-tuple-element.181, f32[8,128,512]{1,2,0:T(8,128)} %get-tuple-element.179, s32[]{:T(128)S(6)} %copy.67), kind=kOutput, calls=%fused_computation.22.clone.1 | convolution fusion | flops 1611137024 | bytes 4464644 | tf_op jit(solution)/shard_map/while/body/eval_jaxpr/dot_general | solution.py:40
  69.2 5.6 %fusion.88 = f32[8,128,512]{1,2,0:T(8,128)} fusion(f32[8,128,512]{1,2,0:T(8,128)} %get-tuple-element.170, s32[]{:T(128)S(6)} %copy.67, f32[512,2048]{1,0:T(8,128)S(1)} %fusion.86, f32[512,2048]{1,0:T(8,128)S(1)} %fusion.87, f32[2048]{0:T(1024)S(1)} %get-tuple-element.180, s32[2048]{0:T(1024)S(1)} %get-tuple-element.182, ...), kind=kOutput, calls=%fused_computation.10.clone.1 | convolution fusion | flops 1614872576 | bytes 8945668 | tf_op jit(solution)/shard_map/while/body/eval_jaxpr/dot_general | solution.py:47
  79.3 4.6 %fusion.87 = f32[512,2048]{1,0:T(8,128)S(1)} fusion(s32[2048]{0:T(1024)S(1)} %get-tuple-element.181, f32[8,128,512]{1,2,0:T(8,128)} %get-tuple-element.179, s32[]{:T(128)S(6)} %copy.67), kind=kOutput, calls=%fused_computation.22.clone.1 | convolution fusion | flops 1611137024 | bytes 4464644 | tf_op jit(solution)/shard_map/while/body/eval_jaxpr/dot_general | solution.py:40
  83.9 5.6 %fusion.88 = f32[8,128,512]{1,2,0:T(8,128)} fusion(f32[8,128,512]{1,2,0:T(8,128)} %get-tuple-element.170, s32[]{:T(128)S(6)} %copy.67, f32[512,2048]{1,0:T(8,128)S(1)} %fusion.86, f32[512,2048]{1,0:T(8,128)S(1)} %fusion.87, f32[2048]{0:T(1024)S(1)} %get-tuple-element.180, s32[2048]{0:T(1024)S(1)} %get-tuple-element.182, ...), kind=kOutput, calls=%fused_computation.10.clone.1 | convolution fusion | flops 1614872576 | bytes 8945668 | tf_op jit(solution)/shard_map/while/body/eval_jaxpr/dot_general | solution.py:47
  94.1 4.6 %fusion.87 = f32[512,2048]{1,0:T(8,128)S(1)} fusion(s32[2048]{0:T(1024)S(1)} %get-tuple-element.181, f32[8,128,512]{1,2,0:T(8,128)} %get-tuple-element.179, s32[]{:T(128)S(6)} %copy.67), kind=kOutput, calls=%fused_computation.22.clone.1 | convolution fusion | flops 1611137024 | bytes 4464644 | tf_op jit(solution)/shard_map/while/body/eval_jaxpr/dot_general | solution.py:40
  98.7 5.6 %fusion.88 = f32[8,128,512]{1,2,0:T(8,128)} fusion(f32[8,128,512]{1,2,0:T(8,128)} %get-tuple-element.170, s32[]{:T(128)S(6)} %copy.67, f32[512,2048]{1,0:T(8,128)S(1)} %fusion.86, f32[512,2048]{1,0:T(8,128)S(1)} %fusion.87, f32[2048]{0:T(1024)S(1)} %get-tuple-element.180, s32[2048]{0:T(1024)S(1)} %get-tuple-element.182, ...), kind=kOutput, calls=%fused_computation.10.clone.1 | convolution fusion | flops 1614872576 | bytes 8945668 | tf_op jit(solution)/shard_map/while/body/eval_jaxpr/dot_general | solution.py:47
  108.9 4.6 %fusion.87 = f32[512,2048]{1,0:T(8,128)S(1)} fusion(s32[2048]{0:T(1024)S(1)} %get-tuple-element.181, f32[8,128,512]{1,2,0:T(8,128)} %get-tuple-element.179, s32[]{:T(128)S(6)} %copy.67), kind=kOutput, calls=%fused_computation.22.clone.1 | convolution fusion | flops 1611137024 | bytes 4464644 | tf_op jit(solution)/shard_map/while/body/eval_jaxpr/dot_general | solution.py:40
  113.5 5.6 %fusion.88 = f32[8,128,512]{1,2,0:T(8,128)} fusion(f32[8,128,512]{1,2,0:T(8,128)} %get-tuple-element.170, s32[]{:T(128)S(6)} %copy.67, f32[512,2048]{1,0:T(8,128)S(1)} %fusion.86, f32[512,2048]{1,0:T(8,128)S(1)} %fusion.87, f32[2048]{0:T(1024)S(1)} %get-tuple-element.180, s32[2048]{0:T(1024)S(1)} %get-tuple-element.182, ...), kind=kOutput, calls=%fused_computation.10.clone.1 | convolution fusion | flops 1614872576 | bytes 8945668 | tf_op jit(solution)/shard_map/while/body/eval_jaxpr/dot_general | solution.py:47
  123.6 4.6 %fusion.87 = f32[512,2048]{1,0:T(8,128)S(1)} fusion(s32[2048]{0:T(1024)S(1)} %get-tuple-element.181, f32[8,128,512]{1,2,0:T(8,128)} %get-tuple-element.179, s32[]{:T(128)S(6)} %copy.67), kind=kOutput, calls=%fused_computation.22.clone.1 | convolution fusion | flops 1611137024 | bytes 4464644 | tf_op jit(solution)/shard_map/while/body/eval_jaxpr/dot_general | solution.py:40
  128.2 5.6 %fusion.88 = f32[8,128,512]{1,2,0:T(8,128)} fusion(f32[8,128,512]{1,2,0:T(8,128)} %get-tuple-element.170, s32[]{:T(128)S(6)} %copy.67, f32[512,2048]{1,0:T(8,128)S(1)} %fusion.86, f32[512,2048]{1,0:T(8,128)S(1)} %fusion.87, f32[2048]{0:T(1024)S(1)} %get-tuple-element.180, s32[2048]{0:T(1024)S(1)} %get-tuple-element.182, ...), kind=kOutput, calls=%fused_computation.10.clone.1 | convolution fusion | flops 1614872576 | bytes 8945668 | tf_op jit(solution)/shard_map/while/body/eval_jaxpr/dot_general | solution.py:47
  138.4 4.6 %fusion.87 = f32[512,2048]{1,0:T(8,128)S(1)} fusion(s32[2048]{0:T(1024)S(1)} %get-tuple-element.181, f32[8,128,512]{1,2,0:T(8,128)} %get-tuple-element.179, s32[]{:T(128)S(6)} %copy.67), kind=kOutput, calls=%fused_computation.22.clone.1 | convolution fusion | flops 1611137024 | bytes 4464644 | tf_op jit(solution)/shard_map/while/body/eval_jaxpr/dot_general | solution.py:40
  143.0 5.6 %fusion.88 = f32[8,128,512]{1,2,0:T(8,128)} fusion(f32[8,128,512]{1,2,0:T(8,128)} %get-tuple-element.170, s32[]{:T(128)S(6)} %copy.67, f32[512,2048]{1,0:T(8,128)S(1)} %fusion.86, f32[512,2048]{1,0:T(8,128)S(1)} %fusion.87, f32[2048]{0:T(1024)S(1)} %get-tuple-element.180, s32[2048]{0:T(1024)S(1)} %get-tuple-element.182, ...), kind=kOutput, calls=%fused_computation.10.clone.1 | convolution fusion | flops 1614872576 | bytes 8945668 | tf_op jit(solution)/shard_map/while/body/eval_jaxpr/dot_general | solution.py:47
  172.3 9.2 %all-to-all-start = ((f32[32,4,8,512]{3,1,2,0:T(4,128)}), f32[32,4,8,512]{3,1,2,0:T(4,128)S(1)}, u32[]{:S(2)}, u32[]{:S(2)}) async-start(f32[32,4,8,512]{3,1,2,0:T(4,128)} %constant_dynamic-update-slice_fusion), calls=%async_computation | async-start | bytes 4194304 | tf_op jit(solution)/shard_map/all_to_all | solution.py:84
  181.7 28.7 %all-to-all-done = f32[32,4,8,512]{3,1,2,0:T(4,128)S(1)} async-done(((f32[32,4,8,512]{3,1,2,0:T(4,128)}), f32[32,4,8,512]{3,1,2,0:T(4,128)S(1)}, u32[]{:S(2)}, u32[]{:S(2)}) %all-to-all-start) | async-done | bytes 2097184 | tf_op jit(solution)/shard_map/all_to_all | solution.py:84
  232.3 30.8 %copy.55 = f32[4,8,16384]{0,1,2:T(8,128)} copy(f32[4,8,16384]{2,0,1:T(4,128)S(1)} %fusion.54) | data formatting | bytes 4194304
  263.1 41.7 %reshape.34 = f32[16384,32]{1,0:T(8,128)} reshape(f32[16384,8,4]{2,1,0:T(8,128)} %bitcast.49) | data formatting | bytes 4194304
  308.3 96.8 %reduce-scatter.4.cloned.1.call-done = f32[512,32]{1,0:T(8,128)} async-done(((f32[16384,32]{1,0:T(8,128)}), f32[512,32]{1,0:T(8,128)}) %reduce-scatter.4.cloned.1.call-update) | async-done | bytes 65552
  (91 shorter events, 103.1 us)
Async XLA Ops:
  7.2 141.4 %copy-start = (f32[128,128]{1,0:T(8,128)S(1)}, f32[128,128]{1,0:T(8,128)}, u32[]{:S(2)}) copy-start(f32[128,128]{1,0:T(8,128)} %param.15) | copy-start | bytes 196612
  9.2 12.1 %copy-start.5 = (s32[3,2048]{1,0:T(4,128)S(1)}, s32[3,2048]{1,0:T(4,128)}, u32[]{:S(2)}) copy-start(s32[3,2048]{1,0:T(4,128)} %param.13) | copy-start | bytes 73732
  9.2 18.1 %copy-start.6 = (f32[128]{0:T(128)S(1)}, f32[128]{0:T(128)}, u32[]{:S(2)}) copy-start(f32[128]{0:T(128)} %param.12) | copy-start | bytes 1540
  9.2 18.1 %copy-start.7 = (f32[128]{0:T(128)S(1)}, f32[128]{0:T(128)}, u32[]{:S(2)}) copy-start(f32[128]{0:T(128)} %param.11) | copy-start | bytes 1540
  9.3 3.1 collective-permute-start.1
  11.0 4.4 %collective-permute-start = (f32[128,8,1]{0,2,1:T(1,128)S(1)}, f32[128,8,1]{0,2,1:T(1,128)S(1)}, u32[]{:S(2)}, u32[]{:S(2)}) collective-permute-start(f32[128,8,1]{0,2,1:T(1,128)S(1)} %get-tuple-element.114), channel_id=1, source_target_pairs={{8,0},{16,8},{24,16},{32,24},{40,32},{48,40},{56,48},{64,56},{72,6... | collective-permute-start | bytes 12296 | tf_op jit(solution)/shard_map/ppermute | solution.py:20
  15.5 9.6 %collective-permute-start.2 = (f32[128,1,514]{0,2,1:T(8,128)S(1)}, f32[128,1,514]{0,2,1:T(8,128)S(1)}, u32[]{:S(2)}, u32[]{:S(2)}) collective-permute-start(f32[128,1,514]{0,2,1:T(8,128)S(1)} %get-tuple-element.109), channel_id=1, source_target_pairs={{1,0},{2,1},{3,2},{4,3},{5,4},{6,5},{7,6},{9,8},{10,9},{11,10},{12... | collective-permute-start | bytes 789512 | tf_op jit(solution)/shard_map/ppermute | solution.py:20
  17.5 9.9 %collective-permute-start.3 = (f32[128,1,514]{0,2,1:T(8,128)S(1)}, f32[128,1,514]{0,2,1:T(8,128)S(1)}, u32[]{:S(2)}, u32[]{:S(2)}) collective-permute-start(f32[128,1,514]{0,2,1:T(8,128)S(1)} %get-tuple-element.110), channel_id=1, source_target_pairs={{0,1},{1,2},{2,3},{3,4},{4,5},{5,6},{6,7},{8,9},{9,10},{10,11},{11... | collective-permute-start | bytes 789512 | tf_op jit(solution)/shard_map/ppermute | solution.py:18
  21.4 9.1 %copy-start.4 = (f32[2048]{0:T(1024)S(1)}, f32[2048]{0:T(1024)}, u32[]{:S(2)}) copy-start(f32[2048]{0:T(1024)} %param.14) | copy-start | bytes 24580
  172.3 9.2 %copy-start.8 = (f32[128]{0:T(128)S(1)}, f32[128]{0:T(128)}, u32[]{:S(2)}) copy-start(f32[128]{0:T(128)} %param.16) | copy-start | bytes 1540
  172.3 9.3 %copy-start.9 = (s32[128]{0:T(128)S(1)}, s32[128]{0:T(128)}, u32[]{:S(2)}) copy-start(s32[128]{0:T(128)} %param.17) | copy-start | bytes 1540
  172.3 38.1 %all-to-all-start = ((f32[32,4,8,512]{3,1,2,0:T(4,128)}), f32[32,4,8,512]{3,1,2,0:T(4,128)S(1)}, u32[]{:S(2)}, u32[]{:S(2)}) async-start(f32[32,4,8,512]{3,1,2,0:T(4,128)} %constant_dynamic-update-slice_fusion), calls=%async_computation | async-start | bytes 4194304 | tf_op jit(solution)/shard_map/all_to_all | solution.py:84
  181.5 223.6 %reduce-scatter.4.cloned.1.call-start = ((), (), s32[]{:S(2)}) async-start(), calls=%async_computation.2 | async-start | bytes 8650752
  218.8 2.9 copy-start.1
  224.3 2.9 copy-start.2
  304.7 1.6 copy-start.3
Sparse Core Ops, SparseCore 0:
  304.9 100.1 reduce-scatter.3
